TPU v7x, 32 devices: a whole 2x2x4 slice. The times are simulated.
32 devices in a mesh: pb: 4 (over y, x), ka: 8 (over z, core).
Axes of the slice: x: 2, y: 2, z: 4, core: 2. Of those that a mesh axis runs over, the one named last changes fastest.
Arguments:
- queries: bfloat16 [4096, 512], P('pb'), may hold values from -100 to 100
- keys: bfloat16 [4096, 512], P('ka'), may hold values from -100 to 100
- values: bfloat16 [4096, 512], P('ka'), may hold values from -6 to 6
Outputs:
- attended: bfloat16 [4096, 512], P(('pb', 'ka'))
All inputs are finite; a program needn't handle non-finite values.
Results may differ from a plain program's by a relative error of at most 0.005.
Values sent between devices are 32-bit elements; how exact they have to be, the bound alone decides.
No kernel may reach another device: no remote copies, remote signals or barrier semaphores. Data moves between devices by JAX's collectives and lax.ppermute only.
A program may use at most 64 MiB of HBM per device.

v0:
```python
import math

import jax
import jax.numpy as jnp
from jax import lax
from jax.sharding import PartitionSpec as P

H = 4
DH = 128
ITERS = 3


def merged(part, axis, combine):
    gathered = jax.tree.map(lambda a: lax.all_gather(a, axis), part)

    def take(source):
        return jax.tree.map(lambda a: lax.dynamic_index_in_dim(a, source, 0, False), gathered)

    return lax.fori_loop(
        1, lax.axis_size(axis), lambda source, state: combine(state, take(source)), take(0)
    )


def merge_stats(first, second):
    peak = jnp.maximum(first[0], second[0])
    total = first[1] * jnp.exp(first[0] - peak) + second[1] * jnp.exp(second[0] - peak)
    return (peak, total)


def over_queries(peak, total):
    global_peak, whole = merged((peak, total), "pb", merge_stats)
    return global_peak + jnp.log(whole)


def over_keys(peak, total):
    global_peak, whole = merged((peak, total), "ka", merge_stats)
    return global_peak + jnp.log(whole)


def body(queries, keys, values):
    q_count = queries.shape[0]
    k_count = keys.shape[0]
    factor = 1.0 / math.sqrt(DH)
    head_queries = queries.reshape(q_count, H, DH).transpose(1, 0, 2)
    head_keys = keys.reshape(k_count, H, DH).transpose(1, 0, 2)
    head_values = values.reshape(k_count, H, DH).transpose(1, 0, 2)

    def head_scores(query_part, index):
        return (
            lax.dot_general(
                query_part,
                head_keys[index],
                (((1,), (1,)), ((), ())),
                preferred_element_type=jnp.float32,
            )
            * factor
        )

    row_pot = jnp.zeros((H, q_count), jnp.float32)
    col_pot = jnp.zeros((H, k_count), jnp.float32)
    for step in range(ITERS):
        peaks = []
        totals = []
        for index in range(H):
            shifted = head_scores(head_queries[index], index) - row_pot[index][:, None]
            peak = jnp.max(shifted, axis=0)
            peaks.append(peak)
            totals.append(jnp.sum(jnp.exp(shifted - peak[None, :]), axis=0))
        col_pot = over_queries(jnp.stack(peaks), jnp.stack(totals))
        peaks = []
        totals = []
        for index in range(H):
            shifted = head_scores(head_queries[index], index) - col_pot[index][None, :]
            peak = jnp.max(shifted, axis=1)
            peaks.append(peak)
            totals.append(jnp.sum(jnp.exp(shifted - peak[:, None]), axis=1))
        row_pot = over_keys(jnp.stack(peaks), jnp.stack(totals))
    pieces = []
    for index in range(H):
        query_part = head_queries[index]
        pot_part = row_pot[index]
        scores = head_scores(query_part, index)
        weights = jnp.exp(scores - pot_part[:, None] - col_pot[index][None, :]).astype(jnp.bfloat16)
        pieces.append(jnp.dot(weights, head_values[index], preferred_element_type=jnp.float32))
    partial_sum = jnp.concatenate(pieces, axis=1)
    summed = lax.psum_scatter(partial_sum, "ka", scatter_dimension=0, tiled=True)
    return summed.astype(jnp.bfloat16)


def solution(mesh):
    in_specs = (P("pb", None), P("ka", None), P("ka", None))
    out_specs = P(("pb", "ka"), None)
    return jax.shard_map(body, mesh=mesh, in_specs=in_specs, out_specs=out_specs, check_vma=False)
```

profile of v0, /device:TPU:0, one launch (start us, length us, event | category | flops | bytes accessed | tf_op | source)
XLA Modules:
  0.0 232.6 jit_solution(6201432794694503613)
XLA Ops:
  6.5 1.3 copy.24
  7.8 1.7 copy.22
  10.9 1.5 fusion.33
  12.5 9.7 %all-gather.12 = f32[4,4,512]{2,1,0:T(4,128)S(1)} all-gather(f32[1,4,512]{2,1,0:T(4,128)S(1)} %maximum_bitcast_fusion.6), channel_id=2, replica_groups=mesh['pb'=4,'ka'=8] {'pb'}, dimensions={0}, use_global_device_ids=true | all-gather | bytes 40960 | tf_op jit(solution)/shard_map/all_gather | solution.py:14
  23.6 8.2 %all-gather.13 = f32[4,4,512]{2,1,0:T(4,128)S(1)} all-gather(f32[1,4,512]{2,1,0:T(4,128)S(1)} %maximum_bitcast_fusion.7), channel_id=3, replica_groups=mesh['pb'=4,'ka'=8] {'pb'}, dimensions={0}, use_global_device_ids=true | all-gather | bytes 40960 | tf_op jit(solution)/shard_map/all_gather | solution.py:14
  32.0 2.0 subtract_reduce_fusion.16
  35.3 1.1 copy-done.15
  38.7 14.3 %all-gather.14 = f32[8,4,1024]{2,1,0:T(4,128)S(1)} all-gather(f32[1,4,1024]{2,1,0:T(4,128)S(1)} %maximum_bitcast_fusion), channel_id=4, replica_groups=mesh['pb'=4,'ka'=8] {'ka'}, dimensions={0}, use_global_device_ids=true | all-gather | bytes 147456 | tf_op jit(solution)/shard_map/all_gather | solution.py:14
  53.0 14.0 %all-gather.15 = f32[8,4,1024]{2,1,0:T(4,128)S(1)} all-gather(f32[1,4,1024]{2,1,0:T(4,128)S(1)} %maximum_bitcast_fusion.1), channel_id=5, replica_groups=mesh['pb'=4,'ka'=8] {'ka'}, dimensions={0}, use_global_device_ids=true | all-gather | bytes 147456 | tf_op jit(solution)/shard_map/all_gather | solution.py:14
  67.4 2.0 subtract_reduce_fusion.12
  70.7 1.1 copy-done.16
  73.6 7.2 %all-gather.16 = f32[4,4,512]{2,1,0:T(4,128)S(1)} all-gather(f32[1,4,512]{2,1,0:T(4,128)S(1)} %maximum_bitcast_fusion.8), channel_id=6, replica_groups=mesh['pb'=4,'ka'=8] {'pb'}, dimensions={0}, use_global_device_ids=true | all-gather | bytes 40960 | tf_op jit(solution)/shard_map/all_gather | solution.py:14
  80.8 8.3 %all-gather.17 = f32[4,4,512]{2,1,0:T(4,128)S(1)} all-gather(f32[1,4,512]{2,1,0:T(4,128)S(1)} %maximum_bitcast_fusion.9), channel_id=7, replica_groups=mesh['pb'=4,'ka'=8] {'pb'}, dimensions={0}, use_global_device_ids=true | all-gather | bytes 40960 | tf_op jit(solution)/shard_map/all_gather | solution.py:14
  89.4 2.0 subtract_reduce_fusion.8
  92.6 1.1 copy-done.17
  96.1 14.0 %all-gather.18 = f32[8,4,1024]{2,1,0:T(4,128)S(1)} all-gather(f32[1,4,1024]{2,1,0:T(4,128)S(1)} %maximum_bitcast_fusion.2), channel_id=8, replica_groups=mesh['pb'=4,'ka'=8] {'ka'}, dimensions={0}, use_global_device_ids=true | all-gather | bytes 147456 | tf_op jit(solution)/shard_map/all_gather | solution.py:14
  110.1 14.0 %all-gather.19 = f32[8,4,1024]{2,1,0:T(4,128)S(1)} all-gather(f32[1,4,1024]{2,1,0:T(4,128)S(1)} %maximum_bitcast_fusion.3), channel_id=9, replica_groups=mesh['pb'=4,'ka'=8] {'ka'}, dimensions={0}, use_global_device_ids=true | all-gather | bytes 147456 | tf_op jit(solution)/shard_map/all_gather | solution.py:14
  124.6 2.0 subtract_reduce_fusion.4
  127.9 1.1 copy-done.18
  130.8 7.2 %all-gather.20 = f32[4,4,512]{2,1,0:T(4,128)S(1)} all-gather(f32[1,4,512]{2,1,0:T(4,128)S(1)} %maximum_bitcast_fusion.10), channel_id=10, replica_groups=mesh['pb'=4,'ka'=8] {'pb'}, dimensions={0}, use_global_device_ids=true | all-gather | bytes 40960 | tf_op jit(solution)/shard_map/all_gather | solution.py:14
  138.0 8.2 %all-gather.21 = f32[4,4,512]{2,1,0:T(4,128)S(1)} all-gather(f32[1,4,512]{2,1,0:T(4,128)S(1)} %maximum_bitcast_fusion.11), channel_id=11, replica_groups=mesh['pb'=4,'ka'=8] {'pb'}, dimensions={0}, use_global_device_ids=true | all-gather | bytes 40960 | tf_op jit(solution)/shard_map/all_gather | solution.py:14
  146.4 2.0 subtract_reduce_fusion
  149.6 1.2 copy-done.19
  153.1 14.0 %all-gather.22 = f32[8,4,1024]{2,1,0:T(4,128)S(1)} all-gather(f32[1,4,1024]{2,1,0:T(4,128)S(1)} %maximum_bitcast_fusion.4), channel_id=12, replica_groups=mesh['pb'=4,'ka'=8] {'ka'}, dimensions={0}, use_global_device_ids=true | all-gather | bytes 147456 | tf_op jit(solution)/shard_map/all_gather | solution.py:14
  167.1 14.2 %all-gather.23 = f32[8,4,1024]{2,1,0:T(4,128)S(1)} all-gather(f32[1,4,1024]{2,1,0:T(4,128)S(1)} %maximum_bitcast_fusion.5), channel_id=13, replica_groups=mesh['pb'=4,'ka'=8] {'ka'}, dimensions={0}, use_global_device_ids=true | all-gather | bytes 147456 | tf_op jit(solution)/shard_map/all_gather | solution.py:14
  182.0 2.4 %fusion.15 = f32[1024,128]{0,1:T(8,128)S(1)} fusion(f32[1024,512]{1,0:T(8,128)} %copy-done.14, f32[1024]{0:T(1024)S(1)} %bitcast.372, f32[512]{0:T(512)S(1)} %bitcast.328, bf16[4,512,128]{1,2,0:T(8,128)(2,1)S(1)} %bitcast.281), kind=kOutput, calls=%fused_computation.86 | convolution fusion | flops 135790592 | bytes 2758656 | tf_op jit(solution)/shard_map/dot_general | solution.py:84
  184.4 0.6 fusion.14
  185.0 0.6 fusion.13
  186.3 1.6 pad_maximum_fusion
  187.9 36.1 %reduce-scatter.2.cloned.1.call-done = f32[128,512]{0,1:T(8,128)} async-done(((f32[1024,512]{0,1:T(8,128)}), f32[128,512]{0,1:T(8,128)}) %reduce-scatter.2.cloned.1.call-update) | async-done | bytes 262160 | tf_op jit(solution)/shard_map/reduce_scatter | solution.py:86
  224.0 1.0 convert_element_type.19
  225.0 0.8 copy.37
  (157 shorter events, 23.4 us)
Async XLA Ops:
  6.5 217.5 %reduce-scatter.2.cloned.1.call-start = ((), (), s32[]{:S(2)}) async-start(), calls=%async_computation.1 | async-start | bytes 2359296 | tf_op jit(solution)/shard_map/reduce_scatter | solution.py:86
  7.8 2.6 %copy-start.20 = (bf16[512,512]{0,1:T(8,128)(2,1)}, bf16[512,512]{0,1:T(8,128)(2,1)S(1)}, u32[]{:S(2)}) copy-start(bf16[512,512]{0,1:T(8,128)(2,1)S(1)} %copy.24) | copy-start | bytes 1572868
  10.0 12.2 %copy-start.14 = (f32[1024,512]{1,0:T(8,128)}, f32[1024,512]{1,0:T(8,128)S(1)}, u32[]{:S(2)}) copy-start(f32[1024,512]{1,0:T(8,128)S(1)} %get-tuple-element.912) | copy-start | bytes 6291460
  10.5 12.1 %copy-start.7 = (f32[1024,512]{1,0:T(8,128)}, f32[1024,512]{1,0:T(8,128)S(1)}, u32[]{:S(2)}) copy-start(f32[1024,512]{1,0:T(8,128)S(1)} %get-tuple-element.914) | copy-start | bytes 6291460
  10.9 12.0 %copy-start = (f32[1024,512]{1,0:T(8,128)}, f32[1024,512]{1,0:T(8,128)S(1)}, u32[]{:S(2)}) copy-start(f32[1024,512]{1,0:T(8,128)S(1)} %get-tuple-element.916) | copy-start | bytes 6291460
  32.0 2.2 copy-start.8
  32.0 2.8 %copy-start.1 = (f32[1024,512]{1,0:T(8,128)S(1)}, f32[1024,512]{1,0:T(8,128)}, u32[]{:S(2)}) copy-start(f32[1024,512]{1,0:T(8,128)} %copy-done) | copy-start | bytes 6291460
  34.8 1.6 copy-start.15
  67.4 2.2 copy-start.9
  67.4 2.8 %copy-start.2 = (f32[1024,512]{1,0:T(8,128)S(1)}, f32[1024,512]{1,0:T(8,128)}, u32[]{:S(2)}) copy-start(f32[1024,512]{1,0:T(8,128)} %copy-done) | copy-start | bytes 6291460
  70.2 1.6 copy-start.16
  89.3 2.2 copy-start.10
  89.4 2.8 %copy-start.3 = (f32[1024,512]{1,0:T(8,128)S(1)}, f32[1024,512]{1,0:T(8,128)}, u32[]{:S(2)}) copy-start(f32[1024,512]{1,0:T(8,128)} %copy-done) | copy-start | bytes 6291460
  92.2 1.6 copy-start.17
  124.6 2.2 copy-start.11
  124.6 2.8 %copy-start.4 = (f32[1024,512]{1,0:T(8,128)S(1)}, f32[1024,512]{1,0:T(8,128)}, u32[]{:S(2)}) copy-start(f32[1024,512]{1,0:T(8,128)} %copy-done) | copy-start | bytes 6291460
  127.4 1.6 copy-start.18
  146.3 2.2 copy-start.12
  146.4 2.8 %copy-start.5 = (f32[1024,512]{1,0:T(8,128)S(1)}, f32[1024,512]{1,0:T(8,128)}, u32[]{:S(2)}) copy-start(f32[1024,512]{1,0:T(8,128)} %copy-done) | copy-start | bytes 6291460
  149.2 1.6 copy-start.19
  152.5 29.3 %copy-start.21 = (bf16[512,512]{1,0:T(8,128)(2,1)S(1)}, bf16[512,512]{1,0:T(8,128)(2,1)}, u32[]{:S(2)}) copy-start(bf16[512,512]{1,0:T(8,128)(2,1)} %param.17) | copy-start | bytes 1572868
  182.0 2.4 %copy-start.13 = (f32[1024,512]{1,0:T(8,128)S(1)}, f32[1024,512]{1,0:T(8,128)}, u32[]{:S(2)}) copy-start(f32[1024,512]{1,0:T(8,128)} %copy-done.7) | copy-start | bytes 6291460
  182.0 3.0 %copy-start.6 = (f32[1024,512]{1,0:T(8,128)S(1)}, f32[1024,512]{1,0:T(8,128)}, u32[]{:S(2)}) copy-start(f32[1024,512]{1,0:T(8,128)} %copy-done) | copy-start | bytes 6291460
Sparse Core Ops, SparseCore 0:
  188.0 35.9 reduce-scatter.1
where the time goes:
time: 233 us
  blocking collectives  133 us (57%)
  waiting for transfers between devices  36.1 us (15%)
  other arithmetic  28.6 us (12%)
  between operations  13.9 us (6%)
  local copies, waits for them, and re-layouts  12.9 us (6%)
  matrix products  7.17 us (3%)
    all_gather x12, blocking collectives, merged(): gathered = jax.tree.map(lambda a: lax.all_gather(a, axis), part)  133 us
    reduce_scatter x1, waiting for transfers between devices, body(): lax.psum_scatter(partial_sum, 'ka', scatter_dimension=0, tiled=True)  36.1 us
    unnamed x47, local copies, waits for them, and re-layouts  12.1 us
    reduce_max x12, other arithmetic, body(): peak = jnp.max(shifted, axis=1)  7.85 us
    reduce_sum x12, other arithmetic, body(): totals.append(jnp.sum(jnp.exp(shifted - peak[:, None]), axis=1))  6.77 us
    reduce_max x8, other arithmetic, body(): peak = jnp.max(shifted, axis=0)  5.23 us
    reduce_sum x12, other arithmetic, body(): totals.append(jnp.sum(jnp.exp(shifted - peak[None, :]), axis=0))  4.85 us
  transfers between devices with their start and end apart: 1, of which 1 were waited for; matrix products, arithmetic and copies ran while one was open for 0% of the time, Pallas kernels for 0%

commit v1 on v0

v1 whole, which is shorter than its diff:
```python
import functools
import math

import jax
import jax.numpy as jnp
from jax import lax
from jax.experimental import pallas as pl
from jax.experimental.pallas import tpu as pltpu
from jax.sharding import PartitionSpec as P

H = 4
DH = 128
ITERS = 3
LANE = 128
CORES = 2
SCALE2 = math.log2(math.e) / math.sqrt(DH)
LOW, HIGH = 1e-13, 1e13
VMEM_BUDGET = 36 * 2**20
F32, BF16 = jnp.float32, jnp.bfloat16
NT = (((1,), (1,)), ((), ()))


def merged(part, axis, combine):
    gathered = jax.tree.map(lambda a: lax.all_gather(a, axis), part)

    def take(source):
        return jax.tree.map(lambda a: lax.dynamic_index_in_dim(a, source, 0, False), gathered)

    return lax.fori_loop(
        1, lax.axis_size(axis), lambda source, state: combine(state, take(source)), take(0)
    )


def merge_stats(first, second):
    peak = jnp.maximum(first[0], second[0])
    total = first[1] * jnp.exp(first[0] - peak) + second[1] * jnp.exp(second[0] - peak)
    return (peak, total)


def merged_log(peak, total, axis):
    global_peak, whole = merged((peak, total), axis, merge_stats)
    return global_peak + jnp.log(whole)


def general_body(queries, keys, values):
    q_count = queries.shape[0]
    k_count = keys.shape[0]
    factor = 1.0 / math.sqrt(DH)
    head_queries = queries.reshape(q_count, H, DH).transpose(1, 0, 2)
    head_keys = keys.reshape(k_count, H, DH).transpose(1, 0, 2)
    head_values = values.reshape(k_count, H, DH).transpose(1, 0, 2)

    def head_scores(query_part, index):
        dots = lax.dot_general(query_part, head_keys[index], NT, preferred_element_type=F32)
        return dots * factor

    row_pot = jnp.zeros((H, q_count), F32)
    col_pot = jnp.zeros((H, k_count), F32)
    for step in range(ITERS):
        peaks = []
        totals = []
        for index in range(H):
            shifted = head_scores(head_queries[index], index) - row_pot[index][:, None]
            peak = jnp.max(shifted, axis=0)
            peaks.append(peak)
            totals.append(jnp.sum(jnp.exp(shifted - peak[None, :]), axis=0))
        col_pot = merged_log(jnp.stack(peaks), jnp.stack(totals), "pb")
        peaks = []
        totals = []
        for index in range(H):
            shifted = head_scores(head_queries[index], index) - col_pot[index][None, :]
            peak = jnp.max(shifted, axis=1)
            peaks.append(peak)
            totals.append(jnp.sum(jnp.exp(shifted - peak[:, None]), axis=1))
        row_pot = merged_log(jnp.stack(peaks), jnp.stack(totals), "ka")
    pieces = []
    for index in range(H):
        scores = head_scores(head_queries[index], index)
        shifted = scores - row_pot[index][:, None] - col_pot[index][None, :]
        weights = jnp.exp(shifted).astype(BF16)
        pieces.append(jnp.dot(weights, head_values[index], preferred_element_type=F32))
    partial_sum = jnp.concatenate(pieces, axis=1)
    summed = lax.psum_scatter(partial_sum, "ka", scatter_dimension=0, tiled=True)
    return summed.astype(BF16)


def to_col(row):
    return jnp.broadcast_to(row, (LANE, LANE)).T


def to_row(col):
    return jnp.broadcast_to(col, (LANE, LANE)).T[0:1]


def in_range(x):
    return (x >= LOW) & (x <= HIGH)


def all_true(mask):
    return jnp.min(jnp.where(mask, 1.0, 0.0)) > 0.5


def split2(x):
    high = x.astype(BF16).astype(F32)
    rows = lax.broadcasted_iota(jnp.int32, (8, x.shape[1]), 0)
    both = jnp.where(rows == 0, high, jnp.where(rows == 1, x - high, 0.0))
    return both.astype(BF16)


def vec_mat(x, mat):
    out = jnp.dot(split2(x), mat, preferred_element_type=F32)
    return out[0:1] + out[1:2]


def inverse(x):
    return jnp.where(in_range(x), 1.0 / x, jnp.nan)


def scores2(q, k):
    return lax.dot_general(q, k, NT, preferred_element_type=F32) * SCALE2


def slow_cols(r_ref, q_ref, k_refs, c_ref):
    rows = q_ref.shape[0]
    for j, k_ref in enumerate(k_refs):
        count = k_ref.shape[0]
        kb = k_ref[...].astype(BF16)

        def block(b, state):
            m, l = state
            at = pl.multiple_of(b * LANE, LANE)
            s = scores2(q_ref[pl.ds(at, LANE), :], kb) - to_col(r_ref[:, pl.ds(at, LANE)])[:, 0:1]
            top = jnp.maximum(m, jnp.max(s, axis=0, keepdims=True))
            l = l * jnp.exp2(m - top) + jnp.sum(jnp.exp2(s - top), axis=0, keepdims=True)
            return top, l

        start = (jnp.full((1, count), -3e38, F32), jnp.zeros((1, count), F32))
        m, l = lax.fori_loop(0, rows // LANE, block, start)
        c_ref[:, j * count : (j + 1) * count] = m + jnp.log2(l)


def slow_block(q, k_refs, c_ref, v_refs=()):
    m = jnp.full((LANE, 1), -3e38, F32)
    l = jnp.zeros((LANE, 1), F32)
    acc = jnp.zeros((LANE, DH), F32)
    for j, k_ref in enumerate(k_refs):
        count = k_ref.shape[0]
        s = scores2(q, k_ref[...].astype(BF16)) - c_ref[:, j * count : (j + 1) * count]
        top = jnp.maximum(m, jnp.max(s, axis=1, keepdims=True))
        e = jnp.exp2(s - top)
        old = jnp.exp2(m - top)
        l = l * old + jnp.sum(e, axis=1, keepdims=True)
        if v_refs:
            v = v_refs[j][...].astype(BF16)
            acc = acc * old + jnp.dot(e.astype(BF16), v, preferred_element_type=F32)
        m = top
    return m, l, acc


def slow_rows(q_ref, k_refs, c_ref, out_ref):
    def block(b, carry):
        at = pl.multiple_of(b * LANE, LANE)
        m, l, _ = slow_block(q_ref[pl.ds(at, LANE), :], k_refs, c_ref)
        out_ref[0:1, pl.ds(at, LANE)] = to_row(l)
        out_ref[1:2, pl.ds(at, LANE)] = to_row(m)
        return carry

    lax.fori_loop(0, q_ref.shape[0] // LANE, block, 0)


def merge_rows(mine_ref, other_ref):
    t1, p1 = mine_ref[0:1, :], mine_ref[1:2, :]
    t2, p2 = other_ref[0:1, :], other_ref[1:2, :]
    peak = jnp.maximum(p1, p2)
    total = t1 * jnp.exp2(p1 - peak) + t2 * jnp.exp2(p2 - peak)
    plain = in_range(total) & (peak == 0.0) & (p1 == p2)
    return jnp.where(plain, total, jnp.nan), peak + jnp.log2(total)


def place_kernel(halves, core_ref, own_ref, mine_ref, other_ref, q_ref):
    rows = own_ref.shape[0]
    half = rows // halves
    core = core_ref[0]
    q_ref[0:rows, :] = own_ref[...]
    for k in range(mine_ref.shape[0]):
        at = (k + 1) * rows
        here = pl.multiple_of(at + core * half, half)
        there = pl.multiple_of(at + (1 - core) * half, half)
        q_ref[pl.ds(here, half), :] = mine_ref[k].astype(BF16)
        q_ref[pl.ds(there, half), :] = other_ref[k].astype(BF16)


def first_kernel(last, *refs):
    if last:
        q_ref, prev_ref, *k_refs = refs[:-5]
        e_ref, t_ref, sums_ref, r_ref, c_ref = refs[-5:]
    else:
        q_ref, prev_ref, *k_refs = refs[:-3]
        e_ref, t_ref, sums_ref = refs[-3:]
    kb = k_refs[-1][...].astype(BF16)
    rows, count = e_ref.shape
    step = 256
    cols = jnp.zeros((8, count), F32)
    for at in range(0, rows, step):
        q = q_ref[at : at + step, :]
        e = jnp.exp2(scores2(q, kb))
        e_ref[at : at + step, :] = e.astype(BF16)
        cols = cols + jnp.sum(e.reshape(step // 8, 8, count), axis=0)
        t_ref[:, at : at + step] = jnp.exp2(scores2(kb, q)).astype(BF16)
    v = inverse(jnp.sum(cols, axis=0, keepdims=True))
    total = prev_ref[0:1, :] + vec_mat(v, t_ref[...])
    sums_ref[0:1, :] = total
    sums_ref[1:2, :] = jnp.zeros_like(total)
    if last:

        @pl.when(jnp.logical_not(all_true(in_range(total))))
        def _():
            r_ref[...] = jnp.zeros_like(r_ref)
            slow_cols(r_ref, q_ref, k_refs, c_ref)
            slow_rows(q_ref, k_refs, c_ref, sums_ref)


def next_kernel(blocks, *refs):
    mine_ref, other_ref, q_ref = refs[:3]
    k_refs = refs[3 : 3 + blocks]
    e_refs = refs[3 + blocks : 3 + 2 * blocks]
    t_refs = refs[3 + 2 * blocks : 3 + 3 * blocks]
    sums_ref, r_ref, c_ref = refs[3 + 3 * blocks :]
    total, log_total = merge_rows(mine_ref, other_ref)
    u = 1.0 / total
    sums = jnp.zeros_like(total)
    for e_ref, t_ref in zip(e_refs, t_refs):
        v = inverse(vec_mat(u, e_ref[...]))
        sums = sums + vec_mat(v, t_ref[...])
    sums_ref[0:1, :] = sums
    sums_ref[1:2, :] = jnp.zeros_like(sums)
    r_ref[...] = log_total

    @pl.when(jnp.logical_not(all_true(in_range(sums))))
    def _():
        slow_cols(r_ref, q_ref, k_refs, c_ref)
        slow_rows(q_ref, k_refs, c_ref, sums_ref)


def last_kernel(blocks, heads, *refs):
    place_ref, mine_ref, other_ref, q_ref = refs[:4]
    k_refs = refs[4 : 4 + blocks]
    e_refs = refs[4 + blocks : 4 + 2 * blocks]
    v_refs = refs[4 + 2 * blocks : 4 + 3 * blocks]
    keep_ref, send_ref, r_ref, c_ref, acc_ref = refs[4 + 3 * blocks :]
    core, chip = place_ref[0], place_ref[1]
    rows = q_ref.shape[0] // heads
    owned = keep_ref.shape[0] // heads
    span = CORES * owned
    total, log_total = merge_rows(mine_ref, other_ref)
    u = 1.0 / total
    starts = [pl.multiple_of(h * rows + chip * span, span) for h in range(heads)]
    acc = jnp.zeros(acc_ref.shape, F32)
    for e_ref, v_ref in zip(e_refs, v_refs):
        v = inverse(vec_mat(u, e_ref[...]))
        count = v.shape[1]
        col = jnp.concatenate([to_col(v[:, at : at + LANE]) for at in range(0, count, LANE)], axis=0)
        high = col.astype(BF16).astype(F32)
        lanes = lax.broadcasted_iota(jnp.int32, col.shape, 1)
        both = jnp.where(lanes % 2 == 0, high, col - high)
        right = jnp.concatenate([(col * v_ref[...]).astype(BF16), both.astype(BF16)], axis=1)
        left = jnp.concatenate([e_ref[pl.ds(at, span), :] for at in starts], axis=0)
        acc = acc + jnp.dot(left, right, preferred_element_type=F32)
    stat = acc[:, DH:]
    stat = stat + pltpu.roll(stat, 1, 1)
    lanes = lax.broadcasted_iota(jnp.int32, stat.shape, 1)
    acc_ref[:, :DH] = acc[:, :DH]
    acc_ref[:, DH:] = jnp.where(lanes < LANE // 2, stat, 0.0)
    r_ref[...] = log_total

    @pl.when(jnp.logical_not(all_true(in_range(stat))))
    def _():
        slow_cols(r_ref, q_ref, k_refs, c_ref)

        def block(b, carry):
            at = pl.multiple_of((b // CORES) * rows + chip * span + (b % CORES) * owned, LANE)
            m, l, num = slow_block(q_ref[pl.ds(at, LANE), :], k_refs, c_ref, v_refs)
            to = pl.multiple_of(b * LANE, LANE)
            acc_ref[pl.ds(to, LANE), :DH] = num
            lanes = lax.broadcasted_iota(jnp.int32, (LANE, LANE), 1)
            acc_ref[pl.ds(to, LANE), DH:] = jnp.where(lanes < LANE // 2, l, m)
            return carry

        lax.fori_loop(0, acc_ref.shape[0] // LANE, block, 0)

    for h in range(heads):
        here = pl.multiple_of(h * span + core * owned, owned)
        there = pl.multiple_of(h * span + (1 - core) * owned, owned)
        keep_ref[h * owned : (h + 1) * owned, :] = acc_ref[pl.ds(here, owned), :]
        send_ref[h * owned : (h + 1) * owned, :] = acc_ref[pl.ds(there, owned), :]


def norm_kernel(mine_ref, other_ref, *out_refs):
    half = DH + LANE // 2
    t1, p1 = mine_ref[:, DH : DH + 1], mine_ref[:, half : half + 1]
    t2, p2 = other_ref[:, DH : DH + 1], other_ref[:, half : half + 1]
    peak = jnp.maximum(p1, p2)
    w1, w2 = jnp.exp2(p1 - peak), jnp.exp2(p2 - peak)
    scale = 1.0 / (t1 * w1 + t2 * w2)
    out = mine_ref[:, :DH] * (w1 * scale) + other_ref[:, :DH] * (w2 * scale)
    owned = out_refs[0].shape[0]
    for h, out_ref in enumerate(out_refs):
        out_ref[...] = out[h * owned : (h + 1) * owned, :]


def join_kernel(place_ref, *refs):
    out_ref = refs[-1]
    for k, ref in enumerate(refs[:-1]):
        at = pl.multiple_of((place_ref[2] ^ k) * DH, DH)
        out_ref[:, pl.ds(at, DH)] = ref[...].astype(BF16)


IN_VMEM = pl.BlockSpec(memory_space=pltpu.VMEM)
IN_SMEM = pl.BlockSpec(memory_space=pltpu.SMEM)


def launch(kernel, outs, args, scalars=0, scratch=(), limit=20, flops=0, transcendentals=0):
    outs = tuple(jax.ShapeDtypeStruct(shape, dtype) for shape, dtype in outs)
    moved = sum(a.size * a.dtype.itemsize for a in args) + sum(
        math.prod(o.shape) * o.dtype.itemsize for o in outs
    )
    return pl.pallas_call(
        kernel,
        out_shape=outs,
        in_specs=[IN_SMEM] * scalars + [IN_VMEM] * (len(args) - scalars),
        out_specs=tuple(IN_VMEM for _ in outs),
        scratch_shapes=scratch,
        compiler_params=pltpu.CompilerParams(vmem_limit_bytes=limit * 2**20),
        cost_estimate=pl.CostEstimate(
            flops=flops, bytes_accessed=moved, transcendentals=transcendentals
        ),
    )(*args)


def head_body(queries, keys, values):
    heads = lax.axis_size("pb")
    chips = lax.axis_size("ka") // CORES
    p = lax.axis_index("pb")
    a = lax.axis_index("ka")
    core, chip = a % CORES, a // CORES
    place = jnp.stack([core, chip, p]).astype(jnp.int32)
    q_rows, k_rows = queries.shape[0], keys.shape[0]
    rows = q_rows * heads
    half = q_rows // CORES
    owned = q_rows // (chips * CORES)

    def swap(x, axis, mask):
        size = lax.axis_size(axis)
        return lax.ppermute(x, axis, [(i, i ^ mask) for i in range(size)])

    def gather_chips(x):
        return [x] + [swap(x, "ka", CORES * k) for k in range(1, chips)]

    mine = []
    for k in range(1, heads):
        part = lax.dynamic_slice(queries, (core * half, (p ^ k) * DH), (half, DH))
        mine.append(swap(part.astype(F32), "pb", k))
    k_blocks = gather_chips(lax.dynamic_slice_in_dim(keys, p * DH, DH, 1).astype(F32))
    mine = jnp.stack(mine)
    other = swap(mine, "ka", 1)
    own = lax.dynamic_slice_in_dim(queries, p * DH, DH, 1)
    (q,) = launch(
        functools.partial(place_kernel, CORES),
        [((rows, DH), BF16)],
        [place, own, mine, other],
        scalars=1,
    )
    v_blocks = gather_chips(lax.dynamic_slice_in_dim(values, p * DH, DH, 1).astype(F32))

    work = [pltpu.VMEM((1, rows), F32), pltpu.VMEM((1, chips * k_rows), F32)]
    sums = jnp.zeros((2, rows), F32)
    e_blocks, t_blocks = [], []
    for j in range(chips):
        last = j == chips - 1
        e, t, sums = launch(
            functools.partial(first_kernel, last),
            [((rows, k_rows), BF16), ((k_rows, rows), BF16), ((2, rows), F32)],
            [q, sums, *(k_blocks if last else k_blocks[j : j + 1])],
            scratch=work if last else (),
            flops=4 * rows * k_rows * DH,
            transcendentals=2 * rows * k_rows,
        )
        e_blocks.append(e)
        t_blocks.append(t)
    for step in range(1, ITERS - 1):
        (sums,) = launch(
            functools.partial(next_kernel, chips),
            [((2, rows), F32)],
            [sums, swap(sums, "ka", 1), q, *k_blocks, *e_blocks, *t_blocks],
            scratch=work,
            flops=64 * rows * chips * k_rows,
        )
    stats = (heads * owned, DH + LANE)
    keep, send = launch(
        functools.partial(last_kernel, chips, heads),
        [(stats, F32), (stats, F32)],
        [place, sums, swap(sums, "ka", 1), q, *k_blocks, *e_blocks, *v_blocks],
        scalars=1,
        scratch=[*work, pltpu.VMEM((CORES * stats[0], stats[1]), F32)],
        flops=64 * rows * chips * k_rows,
    )
    parts = launch(norm_kernel, [((owned, DH), F32)] * heads, [keep, swap(send, "ka", 1)])
    parts = [parts[0]] + [swap(parts[k], "pb", k) for k in range(1, heads)]
    (out,) = launch(join_kernel, [((owned, heads * DH), BF16)], [place, *parts], scalars=1)
    return out


def solution(mesh):
    pb, ka = mesh.shape["pb"], mesh.shape["ka"]

    def body(queries, keys, values):
        rows = pb * queries.shape[0]
        held = 2 * 2 * rows * (ka // CORES) * keys.shape[0]
        powers = pb & (pb - 1) == 0 and ka & (ka - 1) == 0 and ka >= 2 * CORES
        if powers and pb == H and held <= VMEM_BUDGET:
            return head_body(queries, keys, values)
        return general_body(queries, keys, values)

    in_specs = (P("pb", None), P("ka", None), P("ka", None))
    out_specs = P(("pb", "ka"), None)
    return jax.shard_map(body, mesh=mesh, in_specs=in_specs, out_specs=out_specs, check_vma=False)
```

time: 233 us -> 232 us (level)
  Pallas kernels: 0 us -> 172 us
  blocking collectives: 133 us -> 0 us
  other arithmetic: 28.6 us -> 3.07 us
  starting transfers between devices: 0.01 us -> 17.4 us
  between operations: 13.9 us -> 0.12 us
  local copies, waits for them, and re-layouts: 12.9 us -> 3 us
  matrix products: 7.17 us -> 0 us
    pallas_call x0 -> x9, Pallas kernels: none -> 172 us  [launch(): pl.pallas_call(kernel, out_shape=outs, in_specs=[IN_SMEM] * scalars + [IN...]
    all_gather x12 -> x0, blocking collectives: 133 us -> none  [merged(): gathered = jax.tree.map(lambda a: lax.all_gather(a, axis), part)]
    reduce_scatter x1 -> x0, waiting for transfers between devices: 36.1 us -> none  [body(): lax.psum_scatter(partial_sum, 'ka', scatter_dimension=0, tiled=True)]
    ppermute x0 -> x16, waiting for transfers between devices: none -> 35.9 us  [swap(): return lax.ppermute(x, axis, [(i, i ^ mask) for i in range(size)])]
    ppermute x0 -> x16, starting transfers between devices: none -> 17.4 us  [swap(): return lax.ppermute(x, axis, [(i, i ^ mask) for i in range(size)])]
    reduce_max x20 -> x0, other arithmetic: 13.1 us -> none  [the longest x12 7.85 us: body(): peak = jnp.max(shifted, axis=1)]
    reduce_sum x24 -> x0, other arithmetic: 11.6 us -> none  [the longest x12 6.77 us: body(): totals.append(jnp.sum(jnp.exp(shifted - peak[:, None]), axis=1))]
    unnamed x47 -> x6, local copies, waits for them, and re-layouts: 12.1 us -> 2.02 us
  transfers between devices with their start and end apart: 1 -> 16, of which waited for: 1 -> 9; matrix products, arithmetic and copies ran while one was open for 0% -> 1% of each run, Pallas kernels for 0% -> 53%
where the time goes in v1:
time: 232 us
  Pallas kernels  172 us (74%)
  waiting for transfers between devices  35.9 us (15%)
  starting transfers between devices  17.4 us (7%)
  other arithmetic  3.07 us (1%)
  local copies, waits for them, and re-layouts  3 us (1%)
    pallas_call x9, Pallas kernels, launch(): pl.pallas_call(kernel, out_shape=outs, in_specs=[IN_SMEM] * scalars + [IN...  172 us
    ppermute x16, waiting for transfers between devices, swap(): return lax.ppermute(x, axis, [(i, i ^ mask) for i in range(size)])  35.9 us
    ppermute x16, starting transfers between devices, swap(): return lax.ppermute(x, axis, [(i, i ^ mask) for i in range(size)])  17.4 us
  transfers between devices with their start and end apart: 16, of which 9 were waited for; matrix products, arithmetic and copies ran while one was open for 1% of the time, Pallas kernels for 53%

profile of v1, /device:TPU:0, one launch (start us, length us, event | category | flops | bytes accessed | tf_op | source)
XLA Modules:
  0.0 231.7 jit_solution(6271863488391916611)
XLA Ops:
  0.0 1.1 dynamic-slice_convert_fusion.4
  1.1 3.0 %collective-permute-start = (f32[512,128]{1,0:T(8,128)S(1)}, f32[512,128]{1,0:T(8,128)S(1)}, u32[]{:S(2)}, u32[]{:S(2)}) collective-permute-start(f32[512,128]{1,0:T(8,128)S(1)} %get-tuple-element.41), channel_id=1, source_target_pairs={{0,8},{8,0},{16,24},{24,16},{1,9},{9,1},{17,25},{25,17},{2,10},{10... | collective-permute-start | bytes 786440 | tf_op jit(solution)/shard_map/ppermute | solution.py:354
  4.1 1.5 collective-permute-start.1
  5.7 5.6 %collective-permute-done = f32[512,128]{1,0:T(8,128)S(1)} collective-permute-done((f32[512,128]{1,0:T(8,128)S(1)}, f32[512,128]{1,0:T(8,128)S(1)}, u32[]{:S(2)}, u32[]{:S(2)}) %collective-permute-start) | collective-permute-done | bytes 262176 | tf_op jit(solution)/shard_map/ppermute | solution.py:354
  11.3 6.2 %collective-permute-done.1 = f32[512,128]{1,0:T(8,128)S(1)} collective-permute-done((f32[512,128]{1,0:T(8,128)S(1)}, f32[512,128]{1,0:T(8,128)S(1)}, u32[]{:S(2)}, u32[]{:S(2)}) %collective-permute-start.1) | collective-permute-done | bytes 262176 | tf_op jit(solution)/shard_map/ppermute | solution.py:354
  17.7 0.9 dynamic-slice_convert_fusion.1.refs_2_.refs_3_.refs_4_
  18.6 1.6 collective-permute-start.4
  20.2 2.6 %collective-permute-start.5 = (f32[512,128]{1,0:T(8,128)S(1)}, f32[512,128]{1,0:T(8,128)S(1)}, u32[]{:S(2)}, u32[]{:S(2)}) collective-permute-start(f32[512,128]{1,0:T(8,128)S(1)} %dynamic-slice_convert_fusion.1.refs_2_.refs_3_.refs_4_), channel_id=1, source_target_pairs={{0,4},{1,5},{2,6},{3,7},{4,0},{5,1},{6,2},{7,3},{8,12},{9,13},{10,... | collective-permute-start | bytes 786440 | tf_op jit(solution)/shard_map/ppermute | solution.py:354
  23.0 0.9 dynamic-slice_convert_fusion.refs_12_
  24.0 1.8 collective-permute-start.10
  25.7 1.0 constant_dynamic-slice_fusion.own_ref
  26.8 1.9 collective-permute-start.11
  28.7 1.2 shard_map.37.refs_0_.refs_2_.refs_3_
  30.0 2.9 %shard_map.38 = (bf16[4096,512]{1,0:T(8,128)(2,1)S(1)}, bf16[512,4096]{1,0:T(8,128)(2,1)S(1)}, f32[2,4096]{1,0:T(2,128)S(1)}) custom-call(bf16[4096,128]{1,0:T(8,128)(2,1)S(1)} %shard_map.37.refs_0_.refs_2_.refs_3_, f32[2,4096]{1,0:T(2,128)S(1)} %broadcast_in_dim.3.refs_1_, f32[512,128]{1,0:T(8,128)S(1)} %dynamic-slice_convert_fusion.1.refs_2_.refs_3_.refs_4_), custom_call_target="tpu_custom_call" | custom-call | flops 1073741824 | bytes 9764864 | tf_op jit(solution)/shard_map/pallas_call | solution.py:327
  33.0 0.6 collective-permute-start.9
  33.6 2.9 %shard_map.39 = (bf16[4096,512]{1,0:T(8,128)(2,1)S(1)}, bf16[512,4096]{1,0:T(8,128)(2,1)S(1)}, f32[2,4096]{1,0:T(2,128)S(1)}) custom-call(bf16[4096,128]{1,0:T(8,128)(2,1)S(1)} %shard_map.37.refs_0_.refs_2_.refs_3_, f32[2,4096]{1,0:T(2,128)S(1)} %get-tuple-element.23.refs_1_, f32[512,128]{1,0:T(8,128)S(1)} %collective-permute-done.4.refs_2_.refs_3_.refs_4_.refs_5_), custom_call_target="tpu_custom_call" | custom-call | flops 1073741824 | bytes 9764864 | tf_op jit(solution)/shard_map/pallas_call | solution.py:327
  36.5 16.3 %collective-permute-done.5.refs_2_.refs_4_.refs_5_.refs_6_ = f32[512,128]{1,0:T(8,128)S(1)} collective-permute-done((f32[512,128]{1,0:T(8,128)S(1)}, f32[512,128]{1,0:T(8,128)S(1)}, u32[]{:S(2)}, u32[]{:S(2)}) %collective-permute-start.5) | collective-permute-done | bytes 262176 | tf_op jit(solution)/shard_map/ppermute | solution.py:354
  52.9 2.9 %shard_map.40 = (bf16[4096,512]{1,0:T(8,128)(2,1)S(1)}, bf16[512,4096]{1,0:T(8,128)(2,1)S(1)}, f32[2,4096]{1,0:T(2,128)S(1)}) custom-call(bf16[4096,128]{1,0:T(8,128)(2,1)S(1)} %shard_map.37.refs_0_.refs_2_.refs_3_, f32[2,4096]{1,0:T(2,128)S(1)} %get-tuple-element.24.refs_1_, f32[512,128]{1,0:T(8,128)S(1)} %collective-permute-done.5.refs_2_.refs_4_.refs_5_.refs_6_), custom_call_target="tpu_custom_call" | custom-call | flops 1073741824 | bytes 9764864 | tf_op jit(solution)/shard_map/pallas_call | solution.py:327
  55.8 54.1 %shard_map.41 = (bf16[4096,512]{1,0:T(8,128)(2,1)S(1)}, bf16[512,4096]{1,0:T(8,128)(2,1)S(1)}, f32[2,4096]{1,0:T(2,128)S(1)}) custom-call(bf16[4096,128]{1,0:T(8,128)(2,1)S(1)} %shard_map.37.refs_0_.refs_2_.refs_3_, f32[2,4096]{1,0:T(2,128)S(1)} %get-tuple-element.25.refs_1_, f32[512,128]{1,0:T(8,128)S(1)} %dynamic-slice_convert_fusion.1.refs_2_.refs_3_.refs_4_, ...), custom_call_target="tpu_custom_call" | custom-call | flops 1073741824 | bytes 10551296 | tf_op jit(solution)/shard_map/pallas_call | solution.py:327
  110.0 2.0 copy-done.2
  112.0 1.2 collective-permute-done.7.refs_1_
  113.2 57.9 %shard_map.42.refs_1_ = f32[2,4096]{1,0:T(2,128)S(1)} custom-call(f32[2,4096]{1,0:T(2,128)S(1)} %get-tuple-element.26.refs_0_, f32[2,4096]{1,0:T(2,128)S(1)} %collective-permute-done.7.refs_1_, bf16[4096,128]{1,0:T(8,128)(2,1)S(1)} %shard_map.37.refs_0_.refs_2_.refs_3_, f32[512,128]{1,0:T(8,128)S(1)} %dynamic-slice_convert_fusion.1.refs_2_.refs_3_.refs_4_, ...), custom_call_target="tpu_custom_call" | custom-call | flops 536870912 | bytes 35749888 | tf_op jit(solution)/shard_map/pallas_call | solution.py:327
  171.3 1.0 collective-permute-done.8.refs_2_
  172.4 48.3 %shard_map.43 = (f32[512,256]{1,0:T(8,128)S(1)}, f32[512,256]{1,0:T(8,128)S(1)}) custom-call(s32[3]{0:T(128)S(1)} %pad_add_fusion.core_ref.refs_0_.place_ref, f32[2,4096]{1,0:T(2,128)S(1)} %shard_map.42.refs_1_, f32[2,4096]{1,0:T(2,128)S(1)} %collective-permute-done.8.refs_2_, bf16[4096,128]{1,0:T(8,128)(2,1)S(1)} %shard_map.37.refs_0_.refs_2_.refs_3_, ...), custom_call_target="tpu_custom_call" | custom-call | flops 536870912 | bytes 21037068 | tf_op jit(solution)/shard_map/pallas_call | solution.py:327
  221.0 1.7 collective-permute-done.12.other_ref
  223.1 1.3 collective-permute-start.13
  224.4 0.8 collective-permute-start.14
  225.3 1.4 collective-permute-start.15
  226.7 0.8 collective-permute-done.13.refs_1_
  227.5 1.9 collective-permute-done.14.refs_2_
  229.4 1.0 collective-permute-done.15.refs_3_
  230.4 1.2 shard_map.45
  (22 shorter events, 1.3 us)
Async XLA Ops:
  1.1 10.2 %collective-permute-start = (f32[512,128]{1,0:T(8,128)S(1)}, f32[512,128]{1,0:T(8,128)S(1)}, u32[]{:S(2)}, u32[]{:S(2)}) collective-permute-start(f32[512,128]{1,0:T(8,128)S(1)} %get-tuple-element.41), channel_id=1, source_target_pairs={{0,8},{8,0},{16,24},{24,16},{1,9},{9,1},{17,25},{25,17},{2,10},{10... | collective-permute-start | bytes 786440 | tf_op jit(solution)/shard_map/ppermute | solution.py:354
  4.1 13.4 %collective-permute-start.1 = (f32[512,128]{1,0:T(8,128)S(1)}, f32[512,128]{1,0:T(8,128)S(1)}, u32[]{:S(2)}, u32[]{:S(2)}) collective-permute-start(f32[512,128]{1,0:T(8,128)S(1)} %get-tuple-element.43), channel_id=1, source_target_pairs={{0,16},{8,24},{16,0},{24,8},{1,17},{9,25},{17,1},{25,9},{2,18},{10... | collective-permute-start | bytes 786440 | tf_op jit(solution)/shard_map/ppermute | solution.py:354
  5.6 11.9 %collective-permute-start.2 = (f32[512,128]{1,0:T(8,128)S(1)}, f32[512,128]{1,0:T(8,128)S(1)}, u32[]{:S(2)}, u32[]{:S(2)}) collective-permute-start(f32[512,128]{1,0:T(8,128)S(1)} %get-tuple-element.42), channel_id=1, source_target_pairs={{0,24},{8,16},{16,8},{24,0},{1,25},{9,17},{17,9},{25,1},{2,26},{10... | collective-permute-start | bytes 786440 | tf_op jit(solution)/shard_map/ppermute | solution.py:354
  17.6 9.2 %collective-permute-start.3 = (f32[3,512,128]{2,1,0:T(8,128)S(1)}, f32[3,512,128]{2,1,0:T(8,128)}, u32[]{:S(2)}, u32[]{:S(2)}) collective-permute-start(f32[3,512,128]{2,1,0:T(8,128)S(1)} %pad_maximum_fusion.mine_ref), channel_id=1, source_target_pairs={{0,1},{1,0},{2,3},{3,2},{4,5},{5,4},{6,7},{7,6},{8,9},{9,8},{10,11... | collective-permute-start | bytes 2359304 | tf_op jit(solution)/shard_map/ppermute | solution.py:354
  18.6 14.4 %collective-permute-start.4 = (f32[512,128]{1,0:T(8,128)S(1)}, f32[512,128]{1,0:T(8,128)S(1)}, u32[]{:S(2)}, u32[]{:S(2)}) collective-permute-start(f32[512,128]{1,0:T(8,128)S(1)} %dynamic-slice_convert_fusion.1.refs_2_.refs_3_.refs_4_), channel_id=1, source_target_pairs={{0,2},{1,3},{2,0},{3,1},{4,6},{5,7},{6,4},{7,5},{8,10},{9,11},{10,... | collective-permute-start | bytes 786440 | tf_op jit(solution)/shard_map/ppermute | solution.py:354
  20.2 32.6 %collective-permute-start.5 = (f32[512,128]{1,0:T(8,128)S(1)}, f32[512,128]{1,0:T(8,128)S(1)}, u32[]{:S(2)}, u32[]{:S(2)}) collective-permute-start(f32[512,128]{1,0:T(8,128)S(1)} %dynamic-slice_convert_fusion.1.refs_2_.refs_3_.refs_4_), channel_id=1, source_target_pairs={{0,4},{1,5},{2,6},{3,7},{4,0},{5,1},{6,2},{7,3},{8,12},{9,13},{10,... | collective-permute-start | bytes 786440 | tf_op jit(solution)/shard_map/ppermute | solution.py:354
  22.8 33.0 %collective-permute-start.6 = (f32[512,128]{1,0:T(8,128)S(1)}, f32[512,128]{1,0:T(8,128)S(1)}, u32[]{:S(2)}, u32[]{:S(2)}) collective-permute-start(f32[512,128]{1,0:T(8,128)S(1)} %dynamic-slice_convert_fusion.1.refs_2_.refs_3_.refs_4_), channel_id=1, source_target_pairs={{0,6},{1,7},{2,4},{3,5},{4,2},{5,3},{6,0},{7,1},{8,14},{9,15},{10,... | collective-permute-start | bytes 786440 | tf_op jit(solution)/shard_map/ppermute | solution.py:354
  24.0 147.4 %collective-permute-start.10 = (f32[512,128]{1,0:T(8,128)S(1)}, f32[512,128]{1,0:T(8,128)S(1)}, u32[]{:S(2)}, u32[]{:S(2)}) collective-permute-start(f32[512,128]{1,0:T(8,128)S(1)} %dynamic-slice_convert_fusion.refs_12_), channel_id=1, source_target_pairs={{0,4},{1,5},{2,6},{3,7},{4,0},{5,1},{6,2},{7,3},{8,12},{9,13},{10,... | collective-permute-start | bytes 786440 | tf_op jit(solution)/shard_map/ppermute | solution.py:354
  26.8 144.6 %collective-permute-start.11 = (f32[512,128]{1,0:T(8,128)S(1)}, f32[512,128]{1,0:T(8,128)S(1)}, u32[]{:S(2)}, u32[]{:S(2)}) collective-permute-start(f32[512,128]{1,0:T(8,128)S(1)} %dynamic-slice_convert_fusion.refs_12_), channel_id=1, source_target_pairs={{0,6},{1,7},{2,4},{3,5},{4,2},{5,3},{6,0},{7,1},{8,14},{9,15},{10,... | collective-permute-start | bytes 786440 | tf_op jit(solution)/shard_map/ppermute | solution.py:354
  32.9 22.9 %copy-start = (bf16[512,4096]{1,0:T(8,128)(2,1)}, bf16[512,4096]{1,0:T(8,128)(2,1)S(1)}, u32[]{:S(2)}) copy-start(bf16[512,4096]{1,0:T(8,128)(2,1)S(1)} %get-tuple-element.31.refs_11_) | copy-start | bytes 12582916
  33.0 138.4 %collective-permute-start.9 = (f32[512,128]{1,0:T(8,128)S(1)}, f32[512,128]{1,0:T(8,128)S(1)}, u32[]{:S(2)}, u32[]{:S(2)}) collective-permute-start(f32[512,128]{1,0:T(8,128)S(1)} %dynamic-slice_convert_fusion.refs_12_), channel_id=1, source_target_pairs={{0,2},{1,3},{2,0},{3,1},{4,6},{5,7},{6,4},{7,5},{8,10},{9,11},{10,... | collective-permute-start | bytes 786440 | tf_op jit(solution)/shard_map/ppermute | solution.py:354
  55.8 57.4 %copy-start.1 = (bf16[512,4096]{1,0:T(8,128)(2,1)S(1)}, bf16[512,4096]{1,0:T(8,128)(2,1)}, u32[]{:S(2)}) copy-start(bf16[512,4096]{1,0:T(8,128)(2,1)} %copy-done) | copy-start | bytes 12582916
  110.0 2.0 copy-start.2
  112.0 1.2 collective-permute-start.7
  171.1 1.2 collective-permute-start.8
  220.7 2.0 collective-permute-start.12
  223.1 4.3 %collective-permute-start.13 = (f32[128,128]{1,0:T(8,128)S(1)}, f32[128,128]{1,0:T(8,128)S(1)}, u32[]{:S(2)}, u32[]{:S(2)}) collective-permute-start(f32[128,128]{1,0:T(8,128)S(1)} %get-tuple-element.38), channel_id=1, source_target_pairs={{0,8},{8,0},{16,24},{24,16},{1,9},{9,1},{17,25},{25,17},{2,10},{10... | collective-permute-start | bytes 196616 | tf_op jit(solution)/shard_map/ppermute | solution.py:354
  224.4 5.0 %collective-permute-start.14 = (f32[128,128]{1,0:T(8,128)S(1)}, f32[128,128]{1,0:T(8,128)S(1)}, u32[]{:S(2)}, u32[]{:S(2)}) collective-permute-start(f32[128,128]{1,0:T(8,128)S(1)} %get-tuple-element.39), channel_id=1, source_target_pairs={{0,16},{8,24},{16,0},{24,8},{1,17},{9,25},{17,1},{25,9},{2,18},{10... | collective-permute-start | bytes 196616 | tf_op jit(solution)/shard_map/ppermute | solution.py:354
  225.3 5.2 %collective-permute-start.15 = (f32[128,128]{1,0:T(8,128)S(1)}, f32[128,128]{1,0:T(8,128)S(1)}, u32[]{:S(2)}, u32[]{:S(2)}) collective-permute-start(f32[128,128]{1,0:T(8,128)S(1)} %get-tuple-element.40), channel_id=1, source_target_pairs={{0,24},{8,16},{16,8},{24,0},{1,25},{9,17},{17,9},{25,1},{2,26},{10... | collective-permute-start | bytes 196616 | tf_op jit(solution)/shard_map/ppermute | solution.py:354

commit v2 on v0

v2 whole, which is shorter than its diff:
```python
import math

import jax
import jax.numpy as jnp
from jax import lax
from jax.experimental import pallas as pl
from jax.experimental.pallas import tpu as pltpu
from jax.sharding import PartitionSpec as P


H = 4
DH = 128
ITERS = 3
LANE = 128
CORES = 2
SCALE2 = math.log2(math.e) / math.sqrt(DH)
LOW, HIGH = 1e-13, 1e13
VMEM_BUDGET = 36 * 2**20
F32, BF16 = jnp.float32, jnp.bfloat16
NT = (((1,), (1,)), ((), ()))


def merged(part, axis, combine):
    gathered = jax.tree.map(lambda a: lax.all_gather(a, axis), part)

    def take(source):
        return jax.tree.map(lambda a: lax.dynamic_index_in_dim(a, source, 0, False), gathered)

    return lax.fori_loop(
        1, lax.axis_size(axis), lambda source, state: combine(state, take(source)), take(0)
    )


def merge_stats(first, second):
    peak = jnp.maximum(first[0], second[0])
    total = first[1] * jnp.exp(first[0] - peak) + second[1] * jnp.exp(second[0] - peak)
    return (peak, total)


def merged_log(peak, total, axis):
    global_peak, whole = merged((peak, total), axis, merge_stats)
    return global_peak + jnp.log(whole)


def general_body(queries, keys, values):
    q_count = queries.shape[0]
    k_count = keys.shape[0]
    factor = 1.0 / math.sqrt(DH)
    head_queries = queries.reshape(q_count, H, DH).transpose(1, 0, 2)
    head_keys = keys.reshape(k_count, H, DH).transpose(1, 0, 2)
    head_values = values.reshape(k_count, H, DH).transpose(1, 0, 2)

    def head_scores(query_part, index):
        dots = lax.dot_general(query_part, head_keys[index], NT, preferred_element_type=F32)
        return dots * factor

    row_pot = jnp.zeros((H, q_count), F32)
    col_pot = jnp.zeros((H, k_count), F32)
    for _ in range(ITERS):
        peaks = []
        totals = []
        for index in range(H):
            shifted = head_scores(head_queries[index], index) - row_pot[index][:, None]
            peak = jnp.max(shifted, axis=0)
            peaks.append(peak)
            totals.append(jnp.sum(jnp.exp(shifted - peak[None, :]), axis=0))
        col_pot = merged_log(jnp.stack(peaks), jnp.stack(totals), "pb")
        peaks = []
        totals = []
        for index in range(H):
            shifted = head_scores(head_queries[index], index) - col_pot[index][None, :]
            peak = jnp.max(shifted, axis=1)
            peaks.append(peak)
            totals.append(jnp.sum(jnp.exp(shifted - peak[:, None]), axis=1))
        row_pot = merged_log(jnp.stack(peaks), jnp.stack(totals), "ka")
    pieces = []
    for index in range(H):
        scores = head_scores(head_queries[index], index)
        shifted = scores - row_pot[index][:, None] - col_pot[index][None, :]
        weights = jnp.exp(shifted).astype(BF16)
        pieces.append(jnp.dot(weights, head_values[index], preferred_element_type=F32))
    partial_sum = jnp.concatenate(pieces, axis=1)
    summed = lax.psum_scatter(partial_sum, "ka", scatter_dimension=0, tiled=True)
    return summed.astype(BF16)


def to_col(row):
    return jnp.broadcast_to(row, (LANE, LANE)).T


def to_row(col):
    return jnp.broadcast_to(col, (LANE, LANE)).T[0:1]


def in_range(x):
    return (x >= LOW) & (x <= HIGH)


def all_true(mask):
    return jnp.min(jnp.where(mask, 1.0, 0.0)) > 0.5


def split2(x):
    high = x.astype(BF16).astype(F32)
    rows = lax.broadcasted_iota(jnp.int32, (8, x.shape[1]), 0)
    both = jnp.where(rows == 0, high, jnp.where(rows == 1, x - high, 0.0))
    return both.astype(BF16)


def inverse(x):
    return jnp.where(in_range(x), 1.0 / x, jnp.nan)


def scores2(q, k):
    return lax.dot_general(q, k, NT, preferred_element_type=F32) * SCALE2


def slow_cols(r_ref, q_refs, k_ref, count, c_ref):
    for begin in range(0, k_ref.shape[0], count):
        kb = k_ref[begin : begin + count, :]
        state = (jnp.full((1, count), -3e38, F32), jnp.zeros((1, count), F32))
        first = 0
        for q_ref in q_refs:

            def block(b, state, q_ref=q_ref, first=first):
                m, l = state
                at = pl.multiple_of(b * LANE, LANE)
                r = to_col(r_ref[:, pl.ds(first + at, LANE)])[:, 0:1]
                s = scores2(q_ref[pl.ds(at, LANE), :], kb) - r
                top = jnp.maximum(m, jnp.max(s, axis=0, keepdims=True))
                l = l * jnp.exp2(m - top) + jnp.sum(jnp.exp2(s - top), axis=0, keepdims=True)
                return top, l

            state = lax.fori_loop(0, q_ref.shape[0] // LANE, block, state)
            first += q_ref.shape[0]
        c_ref[:, begin : begin + count] = state[0] + jnp.log2(state[1])


def slow_block(q, k_ref, count, c_ref, v_ref=None):
    m = jnp.full((LANE, 1), -3e38, F32)
    l = jnp.zeros((LANE, 1), F32)
    acc = jnp.zeros((LANE, DH), F32)
    for begin in range(0, k_ref.shape[0], count):
        s = scores2(q, k_ref[begin : begin + count, :]) - c_ref[:, begin : begin + count]
        top = jnp.maximum(m, jnp.max(s, axis=1, keepdims=True))
        e = jnp.exp2(s - top)
        old = jnp.exp2(m - top)
        l = l * old + jnp.sum(e, axis=1, keepdims=True)
        if v_ref is not None:
            v = v_ref[begin : begin + count, :]
            acc = acc * old + jnp.dot(e.astype(BF16), v, preferred_element_type=F32)
        m = top
    return m, l, acc


def slow_rows(q_refs, k_ref, count, c_ref, out_ref):
    first = 0
    for q_ref in q_refs:

        def block(b, carry, q_ref=q_ref, first=first):
            at = pl.multiple_of(b * LANE, LANE)
            m, l, _ = slow_block(q_ref[pl.ds(at, LANE), :], k_ref, count, c_ref)
            out_ref[0:1, pl.ds(first + at, LANE)] = to_row(l)
            out_ref[1:2, pl.ds(first + at, LANE)] = to_row(m)
            return carry

        lax.fori_loop(0, q_ref.shape[0] // LANE, block, 0)
        first += q_ref.shape[0]


def merge_rows(mine_ref, other_ref):
    t1, p1 = mine_ref[0:1, :], mine_ref[1:2, :]
    t2, p2 = other_ref[0:1, :], other_ref[1:2, :]
    peak = jnp.maximum(p1, p2)
    total = t1 * jnp.exp2(p1 - peak) + t2 * jnp.exp2(p2 - peak)
    plain = in_range(total) & (peak == 0.0) & (p1 == p2)
    return jnp.where(plain, total, jnp.nan), peak + jnp.log2(total)


def added(refs):
    out = refs[0][...]
    for ref in refs[1:]:
        out = out + ref[...]
    return out


def place(place_ref, mine_ref, other_ref, q_ref):
    blocks, half, _ = mine_ref.shape
    core = place_ref[0]
    for k in range(blocks):
        here = pl.multiple_of((CORES * k + core) * half, half)
        there = pl.multiple_of((CORES * k + 1 - core) * half, half)
        q_ref[pl.ds(here, half), :] = mine_ref[k].astype(BF16)
        q_ref[pl.ds(there, half), :] = other_ref[k].astype(BF16)


def exponents(q_ref, kb, e_ref, t_ref, cols_ref):
    rows, count = e_ref.shape
    step = min(256, rows)
    cols = jnp.zeros((8, count), F32)
    for at in range(0, rows, step):
        q = q_ref[at : at + step, :]
        e = jnp.exp2(scores2(q, kb))
        cols = cols + jnp.sum(e.reshape(step // 8, 8, count), axis=0)
        e = e.astype(BF16)
        e_ref[at : at + step, :] = e
        t_ref[:, at : at + step] = e.T
    cols_ref[...] = jnp.sum(cols, axis=0, keepdims=True)


def add_rows(sums_ref, v, t_refs, begin):
    v = split2(v)
    at = 0
    for t_ref in t_refs:
        out = jnp.dot(v, t_ref[...], preferred_element_type=F32)
        out = out[0:1] + out[1:2]
        to = slice(at, at + t_ref.shape[1])
        sums_ref[0:1, to] = out if begin else sums_ref[0:1, to] + out
        at += t_ref.shape[1]


def col_sums(u, e_refs):
    at, total = 0, 0.0
    for e_ref in e_refs:
        total = total + jnp.dot(u[:, at : at + e_ref.shape[0]], e_ref[...], preferred_element_type=F32)
        at += e_ref.shape[0]
    return total[0:1] + total[1:2]


def make_kernel(q_refs, k_refs, outs):
    for j, k_parts in enumerate(k_refs):
        kb = added(k_parts).astype(BF16)
        for g, q_ref in enumerate(q_refs):
            exponents(q_ref, kb, *outs[g][j])


def place_kernel(place_ref, mine_ref, other_ref, k_refs, q_ref, outs):
    place(place_ref, mine_ref, other_ref, q_ref)
    make_kernel([q_ref], k_refs, outs)


def early_kernel(place_ref, mine_ref, other_ref, k_refs, t_old, cols_old, q_ref, outs, sums_ref):
    place(place_ref, mine_ref, other_ref, q_ref)
    make_kernel([q_ref], k_refs, outs)
    for j in range(len(k_refs)):
        _, t_ref, cols_ref = outs[0][j]
        total = cols_ref[...]
        for old_ref in cols_old[j]:
            total = total + old_ref[...]
        add_rows(sums_ref, inverse(total), [*t_old[j], t_ref], j == 0)


def late_kernel(q_refs, k_refs, prev_ref, outs, sums_ref, all_ref, r_ref, c_ref):
    count = k_refs[-1][0].shape[0]
    for j, k_parts in enumerate(k_refs):
        all_ref[j * count : (j + 1) * count, :] = added(k_parts).astype(BF16)
    kb = all_ref[all_ref.shape[0] - count :, :]
    total = 0.0
    for g, q_ref in enumerate(q_refs):
        exponents(q_ref, kb, *outs[g][0])
        total = total + outs[g][0][2][...]
    sums_ref[0:1, :] = prev_ref[...]
    sums_ref[1:2, :] = jnp.zeros_like(prev_ref)
    add_rows(sums_ref, inverse(total), [outs[g][0][1] for g in range(len(q_refs))], False)

    @pl.when(jnp.logical_not(all_true(in_range(sums_ref[0:1, :]))))
    def _():
        r_ref[...] = jnp.zeros_like(r_ref)
        slow_cols(r_ref, q_refs, all_ref, count, c_ref)
        slow_rows(q_refs, all_ref, count, c_ref, sums_ref)


def next_kernel(mine_ref, other_ref, q_refs, all_ref, e_refs, t_refs, sums_ref, r_ref, c_ref):
    total, log_total = merge_rows(mine_ref, other_ref)
    u = split2(1.0 / total)
    for j in range(len(e_refs)):
        add_rows(sums_ref, inverse(col_sums(u, e_refs[j])), t_refs[j], j == 0)
    sums_ref[1:2, :] = jnp.zeros_like(total)
    r_ref[...] = log_total

    @pl.when(jnp.logical_not(all_true(in_range(sums_ref[0:1, :]))))
    def _():
        count = e_refs[0][0].shape[1]
        slow_cols(r_ref, q_refs, all_ref, count, c_ref)
        slow_rows(q_refs, all_ref, count, c_ref, sums_ref)


def last_kernel(
    place_ref, mine_ref, other_ref, q_refs, all_ref, e_refs, v_refs,
    keep_ref, send_ref, r_ref, c_ref, acc_ref, v_ref,
):
    core, chip = place_ref[0], place_ref[1]
    owned = keep_ref.shape[0] // H
    span = CORES * owned
    rows = q_refs[0].shape[0]
    blocks = [(g, at) for g, q_ref in enumerate(q_refs) for at in range(0, q_ref.shape[0], rows)]
    total, log_total = merge_rows(mine_ref, other_ref)
    u = split2(1.0 / total)
    acc = jnp.zeros(acc_ref.shape, F32)
    for j in range(len(e_refs)):
        v = inverse(col_sums(u, e_refs[j]))
        count = v.shape[1]
        col = jnp.concatenate([to_col(v[:, at : at + LANE]) for at in range(0, count, LANE)], axis=0)
        high = col.astype(BF16).astype(F32)
        lanes = lax.broadcasted_iota(jnp.int32, col.shape, 1)
        both = jnp.where(lanes % 2 == 0, high, col - high)
        value = added(v_refs[j])
        v_ref[j * count : (j + 1) * count, :] = value.astype(BF16)
        right = jnp.concatenate([(col * value).astype(BF16), both.astype(BF16)], axis=1)
        left = [e_refs[j][g][pl.ds(pl.multiple_of(at + chip * span, span), span), :] for g, at in blocks]
        acc = acc + jnp.dot(jnp.concatenate(left, axis=0), right, preferred_element_type=F32)
    stat = acc[:, DH:]
    stat = stat + pltpu.roll(stat, 1, 1)
    lanes = lax.broadcasted_iota(jnp.int32, stat.shape, 1)
    acc_ref[:, :DH] = acc[:, :DH]
    acc_ref[:, DH:] = jnp.where(lanes < LANE // 2, stat, 0.0)
    r_ref[...] = log_total

    @pl.when(jnp.logical_not(all_true(in_range(stat))))
    def _():
        count = e_refs[0][0].shape[1]
        slow_cols(r_ref, q_refs, all_ref, count, c_ref)
        for h, (g, begin) in enumerate(blocks):

            def block(b, carry, q_ref=q_refs[g], begin=begin, h=h):
                at = pl.multiple_of(begin + chip * span + b * LANE, LANE)
                m, l, num = slow_block(q_ref[pl.ds(at, LANE), :], all_ref, count, c_ref, v_ref)
                to = pl.multiple_of(h * span + b * LANE, LANE)
                acc_ref[pl.ds(to, LANE), :DH] = num
                lanes = lax.broadcasted_iota(jnp.int32, (LANE, LANE), 1)
                acc_ref[pl.ds(to, LANE), DH:] = jnp.where(lanes < LANE // 2, l, m)
                return carry

            lax.fori_loop(0, span // LANE, block, 0)

    for h in range(len(blocks)):
        here = pl.multiple_of(h * span + core * owned, owned)
        there = pl.multiple_of(h * span + (1 - core) * owned, owned)
        keep_ref[h * owned : (h + 1) * owned, :] = acc_ref[pl.ds(here, owned), :]
        send_ref[h * owned : (h + 1) * owned, :] = acc_ref[pl.ds(there, owned), :]


def norm_kernel(mine_ref, other_ref, out_refs):
    half = DH + LANE // 2
    t1, p1 = mine_ref[:, DH : DH + 1], mine_ref[:, half : half + 1]
    t2, p2 = other_ref[:, DH : DH + 1], other_ref[:, half : half + 1]
    peak = jnp.maximum(p1, p2)
    w1, w2 = jnp.exp2(p1 - peak), jnp.exp2(p2 - peak)
    scale = 1.0 / (t1 * w1 + t2 * w2)
    out = mine_ref[:, :DH] * (w1 * scale) + other_ref[:, :DH] * (w2 * scale)
    owned = out_refs[0].shape[0]
    for h, out_ref in enumerate(out_refs):
        out_ref[...] = out[h * owned : (h + 1) * owned, :]


def join_kernel(place_ref, refs, out_ref):
    for k, ref in enumerate(refs):
        at = pl.multiple_of((place_ref[2] ^ k) * DH, DH)
        out_ref[:, pl.ds(at, DH)] = ref[...].astype(BF16)


def shape(dims, dtype=F32):
    return jax.ShapeDtypeStruct(dims, dtype)


def launch(kernel, outs, args, scratch=(), limit=6, flops=0, transcendentals=0):
    return call(kernel, outs, args, scratch, limit, flops, transcendentals)


def call(kernel, outs, args, scratch, limit, flops, transcendentals):
    in_specs = jax.tree.map(
        lambda a: pl.BlockSpec(memory_space=pltpu.SMEM if a.dtype == jnp.int32 else pltpu.VMEM), args
    )
    out_specs = jax.tree.map(lambda o: pl.BlockSpec(memory_space=pltpu.VMEM), outs)
    moved = sum(a.size * a.dtype.itemsize for a in jax.tree.leaves((args, outs)))
    return pl.pallas_call(
        kernel,
        out_shape=outs,
        in_specs=in_specs,
        out_specs=out_specs,
        scratch_shapes=scratch,
        compiler_params=pltpu.CompilerParams(vmem_limit_bytes=limit * 2**20),
        cost_estimate=pl.CostEstimate(
            flops=flops, bytes_accessed=moved, transcendentals=transcendentals
        ),
    )(*args)


def head_body(queries, keys, values):
    chips = lax.axis_size("ka") // CORES
    p = lax.axis_index("pb")
    a = lax.axis_index("ka")
    core, chip = a % CORES, a // CORES
    where = jnp.stack([core, chip, p]).astype(jnp.int32)
    q_rows, k_rows = queries.shape[0], keys.shape[0]
    rows = q_rows * H
    half = q_rows // CORES
    owned = q_rows // (chips * CORES)

    def permute(x, axis, target):
        pairs = [(i, target(i)) for i in range(lax.axis_size(axis))]
        return lax.ppermute(x, axis, [(i, t) for i, t in pairs if t is not None])

    def swap(x, axis, mask):
        return permute(x, axis, lambda i: i ^ mask)

    def inner(i):
        return 0 < i // CORES < chips - 1

    def gather_chips(x):
        far = swap(x, "ka", 2 * CORES)
        middle = permute(x, "ka", lambda i: i ^ (3 * CORES) if inner(i) else None)
        near = swap(x, "ka", CORES)
        relay = permute(far, "ka", lambda i: i ^ CORES if inner(i) else None)
        return [[x], [far], [near], [middle, relay]]

    def head(x, h):
        return lax.dynamic_slice_in_dim(x, h * DH, DH, 1)

    def made(groups, blocks):
        return [
            [(shape((g, k_rows), BF16), shape((k_rows, g), BF16), shape((1, k_rows))) for _ in range(blocks)]
            for g in groups
        ]

    def cost(groups, blocks):
        pairs = sum(groups) * blocks * k_rows
        return dict(flops=4 * pairs * DH, transcendentals=2 * pairs)

    k_blocks = gather_chips(head(keys, p).astype(F32))

    mine = {}
    for k in (3, 1, 2):
        part = lax.dynamic_slice(queries, (core * half, (p ^ k) * DH), (half, DH))
        mine[k] = swap(part.astype(F32), "pb", k)
    mine_b, mine_c = jnp.stack([mine[1], mine[2]]), mine[3][None]
    other_b, other_c = swap(mine_b, "ka", 1), swap(mine_c, "ka", 1)
    q_a = head(queries, p)
    size_a, size_b, size_c = q_rows, 2 * q_rows, q_rows

    (out_a,) = launch(make_kernel, [made([size_a], 1)], [[q_a], k_blocks[:1]], **cost([size_a], 1))
    q_b, out_b = launch(
        place_kernel,
        [shape((size_b, DH), BF16), made([size_b], 1)],
        [where, mine_b, other_b, k_blocks[:1]],
        **cost([size_b], 1),
    )
    early = [[out_a[0][0], out_b[0][0]]]
    for j in (1, 2):
        (out,) = launch(
            make_kernel,
            [made([size_a, size_b], 1)],
            [[q_a, q_b], k_blocks[j : j + 1]],
            **cost([size_a, size_b], 1),
        )
        early.append([out[0][0], out[1][0]])
    q_c, out_c, sums = launch(
        early_kernel,
        [shape((size_c, DH), BF16), made([size_c], 3), shape((1, rows))],
        [where, mine_c, other_c, k_blocks[:3], [[o[1] for o in e] for e in early], [[o[2] for o in e] for e in early]],
        **cost([size_c], 3),
    )
    q_parts = [q_a, q_b, q_c]
    work = [pltpu.VMEM((1, rows), F32), pltpu.VMEM((1, chips * k_rows), F32)]
    out_d, sums, k_all = launch(
        late_kernel,
        [made([size_a, size_b, size_c], 1), shape((2, rows)), shape((chips * k_rows, DH), BF16)],
        [q_parts, k_blocks, sums],
        scratch=work,
        **cost([size_a, size_b, size_c], 1),
    )
    blocks = [early[j] + [out_c[0][j]] for j in range(3)] + [[o[0] for o in out_d]]
    e_blocks = [[o[0] for o in b] for b in blocks]
    t_blocks = [[o[1] for o in b] for b in blocks]

    held, _ = lax.optimization_barrier((values, k_blocks[1]))
    v_blocks = gather_chips(head(held, p).astype(F32))

    for _ in range(1, ITERS - 1):
        (sums,) = launch(
            next_kernel,
            [shape((2, rows))],
            [sums, swap(sums, "ka", 1), q_parts, k_all, e_blocks, t_blocks],
            scratch=work,
            flops=64 * rows * chips * k_rows,
        )
    stats = (H * owned, DH + LANE)
    keep, send = launch(
        last_kernel,
        [shape(stats), shape(stats)],
        [where, sums, swap(sums, "ka", 1), q_parts, k_all, e_blocks, v_blocks],
        scratch=[
            *work,
            pltpu.VMEM((CORES * stats[0], stats[1]), F32),
            pltpu.VMEM((chips * k_rows, DH), BF16),
        ],
        limit=12,
        flops=64 * rows * chips * k_rows,
    )
    (parts,) = launch(norm_kernel, [[shape((owned, DH))] * H], [keep, swap(send, "ka", 1)])
    parts = [parts[0]] + [swap(parts[k], "pb", k) for k in range(1, H)]
    (out,) = launch(join_kernel, [shape((owned, H * DH), BF16)], [where, parts])
    return out


def solution(mesh):
    pb, ka = mesh.shape["pb"], mesh.shape["ka"]

    def body(queries, keys, values):
        rows = pb * queries.shape[0]
        held = 2 * 2 * rows * (ka // CORES) * keys.shape[0]
        if pb == H and ka == 4 * CORES and held <= VMEM_BUDGET:
            return head_body(queries, keys, values)
        return general_body(queries, keys, values)

    in_specs = (P("pb", None), P("ka", None), P("ka", None))
    out_specs = P(("pb", "ka"), None)
    return jax.shard_map(body, mesh=mesh, in_specs=in_specs, out_specs=out_specs, check_vma=False)
```

time: 233 us -> 227 us (0.974)
  Pallas kernels: 0 us -> 168 us
  blocking collectives: 133 us -> 0 us
  other arithmetic: 28.6 us -> 3.06 us
  starting transfers between devices: 0.01 us -> 20.6 us
  between operations: 13.9 us -> 0.22 us
  local copies, waits for them, and re-layouts: 12.9 us -> 0.97 us
  matrix products: 7.17 us -> 0 us
    pallas_call x0 -> x10, Pallas kernels: none -> 168 us  [call(): pl.pallas_call(kernel, out_shape=outs, in_specs=in_specs, out_specs=out_s...]
    all_gather x12 -> x0, blocking collectives: 133 us -> none  [merged(): gathered = jax.tree.map(lambda a: lax.all_gather(a, axis), part)]
    reduce_scatter x1 -> x0, waiting for transfers between devices: 36.1 us -> none  [body(): lax.psum_scatter(partial_sum, 'ka', scatter_dimension=0, tiled=True)]
    ppermute x0 -> x19, waiting for transfers between devices: none -> 34.4 us  [permute(): return lax.ppermute(x, axis, [(i, t) for i, t in pairs if t is not None])]
    ppermute x0 -> x19, starting transfers between devices: none -> 20.6 us  [permute(): return lax.ppermute(x, axis, [(i, t) for i, t in pairs if t is not None])]
    reduce_max x20 -> x0, other arithmetic: 13.1 us -> none  [the longest x12 7.85 us: body(): peak = jnp.max(shifted, axis=1)]
    unnamed x47 -> x0, local copies, waits for them, and re-layouts: 12.1 us -> none
    reduce_sum x24 -> x0, other arithmetic: 11.6 us -> none  [the longest x12 6.77 us: body(): totals.append(jnp.sum(jnp.exp(shifted - peak[:, None]), axis=1))]
  transfers between devices with their start and end apart: 1 -> 19, of which waited for: 1 -> 10; matrix products, arithmetic and copies ran while one was open for 0% -> 1% of each run, Pallas kernels for 0% -> 52%
where the time goes in v2:
time: 227 us
  Pallas kernels  168 us (74%)
  waiting for transfers between devices  34.4 us (15%)
  starting transfers between devices  20.6 us (9%)
  other arithmetic  3.06 us (1%)
    pallas_call x10, Pallas kernels, call(): pl.pallas_call(kernel, out_shape=outs, in_specs=in_specs, out_specs=out_s...  168 us
    ppermute x19, waiting for transfers between devices, permute(): return lax.ppermute(x, axis, [(i, t) for i, t in pairs if t is not None])  34.4 us
    ppermute x19, starting transfers between devices, permute(): return lax.ppermute(x, axis, [(i, t) for i, t in pairs if t is not None])  20.6 us
  transfers between devices with their start and end apart: 19, of which 10 were waited for; matrix products, arithmetic and copies ran while one was open for 1% of the time, Pallas kernels for 52%

profile of v2, /device:TPU:0, one launch (start us, length us, event | category | flops | bytes accessed | tf_op | source)
XLA Modules:
  0.0 227.0 jit_solution(6667675959315524816)
XLA Ops:
  0.0 1.1 dynamic-slice_convert_fusion.1
  1.1 3.0 %collective-permute-start = (f32[512,128]{1,0:T(8,128)S(1)}, f32[512,128]{1,0:T(8,128)S(1)}, u32[]{:S(2)}, u32[]{:S(2)}) collective-permute-start(f32[512,128]{1,0:T(8,128)S(1)} %get-tuple-element.90), channel_id=1, source_target_pairs={{0,8},{8,0},{16,24},{24,16},{1,9},{9,1},{17,25},{25,17},{2,10},{10... | collective-permute-start | bytes 786440 | tf_op jit(solution)/shard_map/ppermute | solution.py:402
  4.1 1.5 collective-permute-start.1
  5.7 5.6 %collective-permute-done = f32[512,128]{1,0:T(8,128)S(1)} collective-permute-done((f32[512,128]{1,0:T(8,128)S(1)}, f32[512,128]{1,0:T(8,128)S(1)}, u32[]{:S(2)}, u32[]{:S(2)}) %collective-permute-start) | collective-permute-done | bytes 262176 | tf_op jit(solution)/shard_map/ppermute | solution.py:402
  11.3 6.2 %collective-permute-done.1 = f32[512,128]{1,0:T(8,128)S(1)} collective-permute-done((f32[512,128]{1,0:T(8,128)S(1)}, f32[512,128]{1,0:T(8,128)S(1)}, u32[]{:S(2)}, u32[]{:S(2)}) %collective-permute-start.1) | collective-permute-done | bytes 262176 | tf_op jit(solution)/shard_map/ppermute | solution.py:402
  17.6 0.9 dynamic-slice_convert_fusion.2.k_refs_0__0_
  18.6 2.7 %collective-permute-start.5 = (f32[512,128]{1,0:T(8,128)S(1)}, f32[512,128]{1,0:T(8,128)S(1)}, u32[]{:S(2)}, u32[]{:S(2)}) collective-permute-start(f32[512,128]{1,0:T(8,128)S(1)} %dynamic-slice_convert_fusion.2.k_refs_0__0_), channel_id=1, source_target_pairs={{0,4},{1,5},{2,6},{3,7},{4,0},{5,1},{6,2},{7,3},{8,12},{9,13},{10,... | collective-permute-start | bytes 786440 | tf_op jit(solution)/shard_map/ppermute | solution.py:402
  21.2 1.6 collective-permute-start.6
  23.5 1.0 constant_dynamic-slice_fusion.q_refs_0_
  24.5 9.8 %collective-permute-done.5.k_refs_0__0_.k_refs_1__0_ = f32[512,128]{1,0:T(8,128)S(1)} collective-permute-done((f32[512,128]{1,0:T(8,128)S(1)}, f32[512,128]{1,0:T(8,128)S(1)}, u32[]{:S(2)}, u32[]{:S(2)}) %collective-permute-start.5) | collective-permute-done | bytes 262176 | tf_op jit(solution)/shard_map/ppermute | solution.py:402
  34.4 0.9 dynamic-slice_convert_fusion.v_refs_0__0_
  36.1 1.3 collective-permute-start.8
  37.4 1.6 shard_map.37
  39.0 1.5 shard_map.39
  40.5 3.6 %collective-permute-start.12 = (f32[512,128]{1,0:T(8,128)S(1)}, f32[512,128]{1,0:T(8,128)S(1)}, u32[]{:S(2)}, u32[]{:S(2)}) collective-permute-start(f32[512,128]{1,0:T(8,128)S(1)} %dynamic-slice_convert_fusion.v_refs_0__0_), channel_id=1, source_target_pairs={{0,2},{1,3},{2,0},{3,1},{4,6},{5,7},{6,4},{7,5},{8,10},{9,11},{10,... | collective-permute-start | bytes 786440 | tf_op jit(solution)/shard_map/ppermute | solution.py:402
  44.1 1.5 shard_map.40
  45.6 0.7 collective-permute-start.13
  46.2 5.0 %collective-permute-done.11.v_refs_1__0_ = f32[512,128]{1,0:T(8,128)S(1)} collective-permute-done((f32[512,128]{1,0:T(8,128)S(1)}, f32[512,128]{1,0:T(8,128)S(1)}, u32[]{:S(2)}, u32[]{:S(2)}) %collective-permute-start.11) | collective-permute-done | bytes 262176 | tf_op jit(solution)/shard_map/ppermute | solution.py:402
  51.3 1.3 collective-permute-start.14
  52.6 3.6 %shard_map.41 = (bf16[1024,128]{1,0:T(8,128)(2,1)S(1)}, bf16[1024,512]{1,0:T(8,128)(2,1)S(1)}, bf16[512,1024]{1,0:T(8,128)(2,1)S(1)}, f32[1,512]{1,0:T(1,128)}, ...) custom-call(s32[3]{0:T(128)S(1)} %pad_add_fusion.place_ref, ...), custom_call_target="tpu_custom_call" | custom-call | flops 805306368 | bytes 17336332 | tf_op jit(solution)/shard_map/pallas_call | solution.py:376
  56.2 54.2 %shard_map.42 = (bf16[1024,512]{1,0:T(8,128)(2,1)S(1)}, bf16[512,1024]{1,0:T(8,128)(2,1)S(1)}, f32[1,512]{1,0:T(1,128)}, bf16[2048,512]{1,0:T(8,128)(2,1)S(1)}, ...) custom-call(bf16[1024,128]{1,0:T(8,128)(2,1)S(1)} %constant_dynamic-, ...), custom_call_target="tpu_custom_call" | custom-call | flops 1073741824 | bytes 11327488 | tf_op jit(solution)/shard_map/pallas_call | solution.py:376
  110.4 1.2 collective-permute-done.9.other_ref
  111.6 55.7 %shard_map.43.mine_ref = f32[2,4096]{1,0:T(2,128)S(1)} custom-call(f32[2,4096]{1,0:T(2,128)S(1)} %get-tuple-element.62.mine_ref, f32[2,4096]{1,0:T(2,128)S(1)} %collective-permute-done.9.other_ref, bf16[1024,128]{1,0:T(8,128)(2,1)S(1)} %constant_dynamic-slice_fusion.q_refs_0_, bf16[2048,128]{1,0:T(8,128)(2,1)S(1)} %get-tuple-element.47.q_refs_1_, ...), custom_call_target="tpu_custom_call" | custom-call | flops 536870912 | bytes 35225600 | tf_op jit(solution)/shard_map/pallas_call | solution.py:376
  167.6 1.0 collective-permute-done.10.other_ref
  168.6 47.5 %shard_map.44 = (f32[512,256]{1,0:T(8,128)S(1)}, f32[512,256]{1,0:T(8,128)S(1)}) custom-call(s32[3]{0:T(128)S(1)} %pad_add_fusion.place_ref, f32[2,4096]{1,0:T(2,128)S(1)} %shard_map.43.mine_ref, f32[2,4096]{1,0:T(2,128)S(1)} %collective-permute-done.10.other_ref, bf16[1024,128]{1,0:T(8,128)(2,1)S(1)} %constant_dynamic-slice_fusion.q_refs_0_, ...), custom_call_target="tpu_custom_call" | custom-call | flops 536870912 | bytes 20774924 | tf_op jit(solution)/shard_map/pallas_call | solution.py:376
  216.4 1.7 collective-permute-done.15.other_ref
  218.6 2.0 collective-permute-start.17
  220.7 1.4 collective-permute-start.18
  222.1 1.0 collective-permute-done.16.refs_1_
  223.1 0.7 collective-permute-done.17.refs_2_
  223.8 2.0 collective-permute-done.18.refs_3_
  225.8 1.2 shard_map.46
  (22 shorter events, 2.6 us)
Async XLA Ops:
  1.1 10.2 %collective-permute-start = (f32[512,128]{1,0:T(8,128)S(1)}, f32[512,128]{1,0:T(8,128)S(1)}, u32[]{:S(2)}, u32[]{:S(2)}) collective-permute-start(f32[512,128]{1,0:T(8,128)S(1)} %get-tuple-element.90), channel_id=1, source_target_pairs={{0,8},{8,0},{16,24},{24,16},{1,9},{9,1},{17,25},{25,17},{2,10},{10... | collective-permute-start | bytes 786440 | tf_op jit(solution)/shard_map/ppermute | solution.py:402
  4.1 13.4 %collective-permute-start.1 = (f32[512,128]{1,0:T(8,128)S(1)}, f32[512,128]{1,0:T(8,128)S(1)}, u32[]{:S(2)}, u32[]{:S(2)}) collective-permute-start(f32[512,128]{1,0:T(8,128)S(1)} %get-tuple-element.91), channel_id=1, source_target_pairs={{0,16},{8,24},{16,0},{24,8},{1,17},{9,25},{17,1},{25,9},{2,18},{10... | collective-permute-start | bytes 786440 | tf_op jit(solution)/shard_map/ppermute | solution.py:402
  5.6 18.8 %collective-permute-start.3 = (f32[512,128]{1,0:T(8,128)S(1)}, f32[512,128]{1,0:T(8,128)S(1)}, u32[]{:S(2)}, u32[]{:S(2)}) collective-permute-start(f32[512,128]{1,0:T(8,128)S(1)} %get-tuple-element.89), channel_id=1, source_target_pairs={{0,24},{8,16},{16,8},{24,0},{1,25},{9,17},{17,9},{25,1},{2,26},{10... | collective-permute-start | bytes 786440 | tf_op jit(solution)/shard_map/ppermute | solution.py:402
  17.5 18.5 %collective-permute-start.2 = (f32[2,512,128]{2,1,0:T(8,128)S(1)}, f32[2,512,128]{2,1,0:T(8,128)S(1)}, u32[]{:S(2)}, u32[]{:S(2)}) collective-permute-start(f32[2,512,128]{2,1,0:T(8,128)S(1)} %pad_maximum_fusion.mine_ref), channel_id=1, source_target_pairs={{0,1},{1,0},{2,3},{3,2},{4,5},{5,4},{6,7},{7,6},{8,9},{9,8},{10,11... | collective-permute-start | bytes 1572872 | tf_op jit(solution)/shard_map/ppermute | solution.py:402
  18.6 15.8 %collective-permute-start.5 = (f32[512,128]{1,0:T(8,128)S(1)}, f32[512,128]{1,0:T(8,128)S(1)}, u32[]{:S(2)}, u32[]{:S(2)}) collective-permute-start(f32[512,128]{1,0:T(8,128)S(1)} %dynamic-slice_convert_fusion.2.k_refs_0__0_), channel_id=1, source_target_pairs={{0,4},{1,5},{2,6},{3,7},{4,0},{5,1},{6,2},{7,3},{8,12},{9,13},{10,... | collective-permute-start | bytes 786440 | tf_op jit(solution)/shard_map/ppermute | solution.py:402
  21.2 19.2 %collective-permute-start.6 = (f32[512,128]{1,0:T(8,128)S(1)}, f32[512,128]{1,0:T(8,128)S(1)}, u32[]{:S(2)}, u32[]{:S(2)}) collective-permute-start(f32[512,128]{1,0:T(8,128)S(1)} %dynamic-slice_convert_fusion.2.k_refs_0__0_), channel_id=1, source_target_pairs={{0,2},{1,3},{2,0},{3,1},{4,6},{5,7},{6,4},{7,5},{8,10},{9,11},{10,... | collective-permute-start | bytes 786440 | tf_op jit(solution)/shard_map/ppermute | solution.py:402
  22.8 33.4 %collective-permute-start.7 = (f32[512,128]{1,0:T(8,128)S(1)}, f32[512,128]{1,0:T(8,128)S(1)}, u32[]{:S(2)}, u32[]{:S(2)}) collective-permute-start(f32[512,128]{1,0:T(8,128)S(1)} %dynamic-slice_convert_fusion.2.k_refs_0__0_), channel_id=1, source_target_pairs={{2,4},{3,5},{4,2},{5,3},{10,12},{11,13},{12,10},{13,11},{18,20},{1... | collective-permute-start | bytes 786440 | tf_op jit(solution)/shard_map/ppermute | solution.py:402
  24.5 21.1 %collective-permute-start.4 = (f32[1,512,128]{2,1,0:T(8,128)S(1)}, f32[1,512,128]{2,1,0:T(8,128)S(1)}, u32[]{:S(2)}, u32[]{:S(2)}) collective-permute-start(f32[1,512,128]{2,1,0:T(8,128)S(1)} %bitcast.6), channel_id=1, source_target_pairs={{0,1},{1,0},{2,3},{3,2},{4,5},{5,4},{6,7},{7,6},{8,9},{9,8},{10,11... | collective-permute-start | bytes 786440 | tf_op jit(solution)/shard_map/ppermute | solution.py:402
  35.3 16.0 %collective-permute-start.11 = (f32[512,128]{1,0:T(8,128)S(1)}, f32[512,128]{1,0:T(8,128)S(1)}, u32[]{:S(2)}, u32[]{:S(2)}) collective-permute-start(f32[512,128]{1,0:T(8,128)S(1)} %dynamic-slice_convert_fusion.v_refs_0__0_), channel_id=1, source_target_pairs={{0,4},{1,5},{2,6},{3,7},{4,0},{5,1},{6,2},{7,3},{8,12},{9,13},{10,... | collective-permute-start | bytes 786440 | tf_op jit(solution)/shard_map/ppermute | solution.py:402
  36.1 20.1 %collective-permute-start.8 = (f32[512,128]{1,0:T(8,128)S(1)}, f32[512,128]{1,0:T(8,128)S(1)}, u32[]{:S(2)}, u32[]{:S(2)}) collective-permute-start(f32[512,128]{1,0:T(8,128)S(1)} %collective-permute-done.5.k_refs_0__0_.k_refs_1__0_), channel_id=1, source_target_pairs={{2,0},{3,1},{4,6},{5,7},{10,8},{11,9},{12,14},{13,15},{18,16},{19,... | collective-permute-start | bytes 786440 | tf_op jit(solution)/shard_map/ppermute | solution.py:402
  40.5 127.1 %collective-permute-start.12 = (f32[512,128]{1,0:T(8,128)S(1)}, f32[512,128]{1,0:T(8,128)S(1)}, u32[]{:S(2)}, u32[]{:S(2)}) collective-permute-start(f32[512,128]{1,0:T(8,128)S(1)} %dynamic-slice_convert_fusion.v_refs_0__0_), channel_id=1, source_target_pairs={{0,2},{1,3},{2,0},{3,1},{4,6},{5,7},{6,4},{7,5},{8,10},{9,11},{10,... | collective-permute-start | bytes 786440 | tf_op jit(solution)/shard_map/ppermute | solution.py:402
  45.6 122.0 %collective-permute-start.13 = (f32[512,128]{1,0:T(8,128)S(1)}, f32[512,128]{1,0:T(8,128)S(1)}, u32[]{:S(2)}, u32[]{:S(2)}) collective-permute-start(f32[512,128]{1,0:T(8,128)S(1)} %dynamic-slice_convert_fusion.v_refs_0__0_), channel_id=1, source_target_pairs={{2,4},{3,5},{4,2},{5,3},{10,12},{11,13},{12,10},{13,11},{18,20},{1... | collective-permute-start | bytes 786440 | tf_op jit(solution)/shard_map/ppermute | solution.py:402
  51.3 116.3 %collective-permute-start.14 = (f32[512,128]{1,0:T(8,128)S(1)}, f32[512,128]{1,0:T(8,128)S(1)}, u32[]{:S(2)}, u32[]{:S(2)}) collective-permute-start(f32[512,128]{1,0:T(8,128)S(1)} %collective-permute-done.11.v_refs_1__0_), channel_id=1, source_target_pairs={{2,0},{3,1},{4,6},{5,7},{10,8},{11,9},{12,14},{13,15},{18,16},{19,... | collective-permute-start | bytes 786440 | tf_op jit(solution)/shard_map/ppermute | solution.py:402
  110.4 1.2 collective-permute-start.9
  167.3 1.3 collective-permute-start.10
  216.1 2.0 collective-permute-start.15
  218.5 4.6 %collective-permute-start.16 = (f32[128,128]{1,0:T(8,128)S(1)}, f32[128,128]{1,0:T(8,128)S(1)}, u32[]{:S(2)}, u32[]{:S(2)}) collective-permute-start(f32[128,128]{1,0:T(8,128)S(1)} %get-tuple-element.86), channel_id=1, source_target_pairs={{0,8},{8,0},{16,24},{24,16},{1,9},{9,1},{17,25},{25,17},{2,10},{10... | collective-permute-start | bytes 196616 | tf_op jit(solution)/shard_map/ppermute | solution.py:402
  218.6 5.2 %collective-permute-start.17 = (f32[128,128]{1,0:T(8,128)S(1)}, f32[128,128]{1,0:T(8,128)S(1)}, u32[]{:S(2)}, u32[]{:S(2)}) collective-permute-start(f32[128,128]{1,0:T(8,128)S(1)} %get-tuple-element.87), channel_id=1, source_target_pairs={{0,16},{8,24},{16,0},{24,8},{1,17},{9,25},{17,1},{25,9},{2,18},{10... | collective-permute-start | bytes 196616 | tf_op jit(solution)/shard_map/ppermute | solution.py:402
  220.7 5.2 %collective-permute-start.18 = (f32[128,128]{1,0:T(8,128)S(1)}, f32[128,128]{1,0:T(8,128)S(1)}, u32[]{:S(2)}, u32[]{:S(2)}) collective-permute-start(f32[128,128]{1,0:T(8,128)S(1)} %get-tuple-element.88), channel_id=1, source_target_pairs={{0,24},{8,16},{16,8},{24,0},{1,25},{9,17},{17,9},{25,1},{2,26},{10... | collective-permute-start | bytes 196616 | tf_op jit(solution)/shard_map/ppermute | solution.py:402
